TPU v7x, 1024 devices: a whole 4x8x16 slice. The times are simulated.
1024 devices in a mesh: dp: 16 (over z), shard: 64 (over y, x, core).
Axes of the slice: x: 4, y: 8, z: 16, core: 2. Of those that a mesh axis runs over, the one named last changes fastest.
Arguments:
- partials: bfloat16 [16, 2, 1024, 8192], P('dp', None, 'shard'), may hold values from -6 to 6
- block_owner: int32 [64], replicated, may hold values from 0 to 63, as said below
- owner_slot: int32 [64], replicated, may hold values from 0 to 0, as said below
- fac_left: float32 [64, 512, 512], P('shard'), may hold values from -6 to 6
- fac_right: float32 [64, 512, 512], P('shard'), may hold values from -6 to 6
- moment: bfloat16 [64, 512, 512], P('shard'), may hold values from -12 to 12
- second: float32 [64, 512, 512], P('shard'), may hold values from 1 to 16
- basis_left: bfloat16 [64, 512, 512], P('shard'), may hold values from -1 to 1, as said below
- basis_right: bfloat16 [64, 512, 512], P('shard'), may hold values from -1 to 1, as said below
Outputs:
- update: bfloat16 [2, 1024, 8192], P(None, 'shard')
- fac_left_new: float32 [64, 512, 512], P('shard')
- fac_right_new: float32 [64, 512, 512], P('shard')
- moment_new: bfloat16 [64, 512, 512], P('shard')
- second_new: float32 [64, 512, 512], P('shard')
Inputs may be any that keep to these rules, and one draw needn't show every extreme that they name: `block_owner`: each owner is named by exactly 1 block. `owner_slot`: the blocks of one owner have distinct slots. `basis_left`: each block is an orthogonal matrix rounded to bfloat16. `basis_right`: each block is an orthogonal matrix rounded to bfloat16.
All inputs are finite; a program needn't handle non-finite values.
Results may differ from a plain program's by a relative error of at most 0.018.
Values may be sent and summed in bfloat16 or wider, within the bound.
A program may use at most 32 MiB of HBM per device.

v0:
```python
import jax
import jax.numpy as jnp
from jax import lax
from jax.sharding import PartitionSpec as P


def in_blocks(shard, dim, count):
    before, after = (shard.shape[:dim], shard.shape[dim + 1 :])
    return jnp.moveaxis(shard.reshape(*before, count, -1, *after), dim, 0)


def sum_at_owner(shard, axis, dim):
    count = lax.axis_size(axis)
    tiles = lax.all_to_all(in_blocks(shard, dim, count), axis, 0, 0, tiled=True)
    return jnp.sum(tiles.astype(jnp.float32), axis=0)


def product(left_side, right_side, form):
    return jnp.einsum(form, left_side, right_side, preferred_element_type=jnp.float32)


def to_pieces(flat_rows, column_count, block_size):
    row_count = flat_rows.shape[1]
    divided = flat_rows.reshape(2, row_count, column_count, block_size)
    return jnp.transpose(divided, (0, 2, 1, 3)).reshape(2 * column_count, row_count * block_size)


def soap_blocks(grads, fac_left, fac_right, moment, second, basis_left, basis_right):
    left_new = 0.95 * fac_left + 0.05 * product(grads, grads, "kij,klj->kil")
    right_new = 0.95 * fac_right + 0.05 * product(grads, grads, "kji,kjl->kil")
    moment_next = (0.9 * moment.astype(jnp.float32) + 0.1 * grads.astype(jnp.float32)).astype(
        jnp.bfloat16
    )

    def rotate_into(matrix):
        rotated_half = product(basis_left, matrix, "kji,kjl->kil").astype(jnp.bfloat16)
        return product(rotated_half, basis_right, "kij,kjl->kil")

    grad_rotated = rotate_into(grads)
    second_next = 0.95 * second + 0.05 * grad_rotated * grad_rotated
    moment_rotated = rotate_into(moment_next)
    scaled = (moment_rotated / (jnp.sqrt(second_next) + 1e-08)).astype(jnp.bfloat16)
    back_half = product(basis_left, scaled, "kij,kjl->kil").astype(jnp.bfloat16)
    update_blocks = product(back_half, basis_right, "kij,klj->kil").astype(jnp.bfloat16)
    return (left_new, right_new, moment_next, second_next, update_blocks)


def shards(
    partials, block_owner, owner_slot, fac_left, fac_right, moment, second, basis_left, basis_right
):
    shard_count = lax.axis_size("shard")
    shard_index = lax.axis_index("shard")
    slot_count = fac_left.shape[0]
    block_size = fac_left.shape[1]
    row_count = partials.shape[2]
    full_width = partials.shape[3]
    column_count = full_width // block_size
    block_count = block_owner.shape[0]
    block_rows = block_count // (2 * column_count)
    sources_row = block_size // row_count
    position = block_owner * slot_count + owner_slot
    own_row = shard_index * row_count // block_size
    first_run = lax.dynamic_slice_in_dim(position, own_row * column_count, column_count)
    second_run = lax.dynamic_slice_in_dim(
        position, (block_rows + own_row) * column_count, column_count
    )
    target_pos = jnp.concatenate([first_run, second_run])
    numbering = jnp.arange(block_count, dtype=jnp.int32)
    selector = (target_pos[:, None] == numbering[None, :]).astype(jnp.bfloat16)
    held_pos = shard_index * slot_count + jnp.arange(slot_count, dtype=jnp.int32)
    held_block = jnp.sum(
        jnp.where(position[None, :] == held_pos[:, None], numbering[None, :], 0), axis=1
    )
    held_row = held_block // column_count % block_rows
    pieces = to_pieces(partials[0], column_count, block_size)
    placed = jnp.einsum("jp,jx->px", selector, pieces, preferred_element_type=jnp.float32)
    local_rows = (
        placed.astype(jnp.bfloat16).reshape(block_count, row_count, block_size).astype(jnp.float32)
    )
    share_rows = sum_at_owner(local_rows.astype(jnp.bfloat16), "dp", 2).astype(jnp.bfloat16)
    arrived_share = lax.all_to_all(share_rows, "shard", split_axis=0, concat_axis=0, tiled=True)
    width = arrived_share.shape[-1]
    grouped = arrived_share.reshape(shard_count, slot_count, row_count, width)
    slot_index = 0
    column = lax.dynamic_slice_in_dim(
        grouped[:, slot_index], held_row[slot_index] * sources_row, sources_row, 0
    )
    blocks = [column.reshape(block_size, width)]
    grad_blocks = lax.all_gather(jnp.stack(blocks), "dp", axis=2, tiled=True)
    left_new, right_new, moment_next, second_next, update_blocks = soap_blocks(
        grad_blocks, fac_left, fac_right, moment, second, basis_left, basis_right
    )
    width = update_blocks.shape[-1]
    slot_index = 0
    target = jnp.zeros((shard_count, row_count, width), jnp.bfloat16)
    rows_out = update_blocks[slot_index].reshape(sources_row, row_count, width)
    target = lax.dynamic_update_slice_in_dim(
        target, rows_out, held_row[slot_index] * sources_row, 0
    )
    returned = [target]
    arrived = lax.all_to_all(
        jnp.stack(returned, axis=1).reshape(shard_count * slot_count, row_count, width),
        "shard",
        split_axis=0,
        concat_axis=0,
        tiled=True,
    )
    width = arrived.shape[-1]
    picked = jnp.einsum(
        "jp,px->jx",
        selector,
        arrived.reshape(block_count, row_count * width),
        preferred_element_type=jnp.float32,
    ).astype(jnp.bfloat16)
    flat_pieces = picked.reshape(2, column_count, row_count, width)
    update = jnp.transpose(flat_pieces, (0, 2, 1, 3)).reshape(2, row_count, full_width)
    return (update, left_new, right_new, moment_next, second_next)


def solution(mesh):
    in_specs = (
        P("dp", None, "shard", None),
        P(),
        P(),
        P("shard", None, None),
        P("shard", None, None),
        P("shard", None, None),
        P("shard", None, None),
        P("shard", None, None),
        P("shard", None, None),
    )
    out_specs = (
        P(None, "shard", None),
        P("shard", None, None),
        P("shard", None, None),
        P("shard", None, None),
        P("shard", None, None),
    )
    return jax.shard_map(shards, mesh=mesh, in_specs=in_specs, out_specs=out_specs, check_vma=False)
```

profile of v0, /device:TPU:1, one launch (start us, length us, event | category | flops | bytes accessed | tf_op | source)
XLA Modules:
  0.0 186.7 jit_solution(6752097138053560596)
XLA Ops:
  0.6 0.0 copy-start
  0.6 0.0 copy-start.3
  0.7 0.0 copy-start.4
  0.7 1.3 copy.45
  1.9 0.3 copy.35
  2.2 0.3 copy.46
  2.6 0.0 copy-done.3
  2.6 0.0 copy-done.4
  2.6 0.6 fusion.27
  3.2 0.1 fusion.28
  3.3 0.1 pad_add_fusion
  3.4 1.5 convolution_convert_fusion
  4.9 2.0 %copy.36 = bf16[64,8192]{0,1:T(8,128)(2,1)S(1)} copy(bf16[64,8192]{1,0:T(8,128)(2,1)} %convolution_convert_fusion) | data formatting | bytes 2097152 | tf_op jit(solution)/shard_map/convert_element_type | solution.py:78
  6.9 1.9 %copy.50 = bf16[16,64,16,32]{1,3,2,0:T(8,128)(2,1)} copy(bf16[16,64,16,32]{1,3,0,2:T(8,128)(2,1)S(1)} %bitcast.86) | data formatting | bytes 2097152 | tf_op jit(solution)/shard_map/transpose | solution.py:9
  8.8 3.9 %reshape.99 = bf16[16,2,16384]{2,1,0:T(2,128)(2,1)S(1)} reshape(bf16[16,16,32,64]{3,2,1,0:T(8,128)(2,1)} %bitcast.87) | data formatting | bytes 2097152
  12.7 64.8 %all_to_all.15 = bf16[16,2,16384]{2,1,0:T(2,128)(2,1)} all-to-all(bf16[16,2,16384]{2,1,0:T(2,128)(2,1)S(1)} %reshape.99), channel_id=1, replica_groups=mesh['dp'=16,'shard'=64] {'dp'}, dimensions={0} | all-to-all | bytes 2097152 | tf_op jit(solution)/shard_map/all_to_all | solution.py:14
  77.5 3.8 %reshape.100 = bf16[16,16,32,64]{3,2,1,0:T(8,128)(2,1)S(1)} reshape(bf16[16,2,16384]{2,1,0:T(2,128)(2,1)} %all_to_all.15) | data formatting | bytes 2097152
  81.3 0.0 copy-start.2
  81.3 0.4 bitcast_reduce_fusion
  81.7 0.3 copy.39
  82.0 0.8 reshape.101
  82.8 0.0 copy-start.5
  82.8 17.3 %all-to-all-start.1 = ((bf16[64,2,256]{2,1,0:T(2,128)(2,1)}), bf16[64,2,256]{2,1,0:T(2,128)(2,1)S(1)}, u32[]{:S(2)}, u32[]{:S(2)}) async-start(bf16[64,2,256]{2,1,0:T(2,128)(2,1)} %reshape.101), calls=%async_computation.1 | async-start | bytes 131072 | tf_op jit(solution)/shard_map/all_to_all | solution.py:81
  102.7 0.0 copy-done.2
  102.7 0.2 copy.34
  103.0 7.2 %all-to-all-done.1 = bf16[64,2,256]{2,1,0:T(2,128)(2,1)S(1)} async-done(((bf16[64,2,256]{2,1,0:T(2,128)(2,1)}), bf16[64,2,256]{2,1,0:T(2,128)(2,1)S(1)}, u32[]{:S(2)}, u32[]{:S(2)}) %all-to-all-start.1) | async-done | bytes 65568 | tf_op jit(solution)/shard_map/all_to_all | solution.py:81
  110.2 0.2 reshape.102
  110.4 0.1 copy.40
  110.5 26.5 %all_gather.3 = bf16[1,512,512]{1,2,0:T(8,128)(2,1)S(1)} all-gather(bf16[1,512,32]{1,2,0:T(8,128)(2,1)S(1)} %copy.40), channel_id=1, replica_groups=mesh['dp'=16,'shard'=64] {'dp'}, dimensions={2}, use_global_device_ids=true | all-gather | bytes 557056 | tf_op jit(solution)/shard_map/all_gather | solution.py:89
  137.0 0.2 add_convert_fusion
  137.2 0.0 copy-done
  137.2 0.0 copy-done.5
  137.2 3.1 %fusion.6 = f32[1,512,512]{2,1,0:T(8,128)} fusion(f32[1,512,512]{2,1,0:T(8,128)} %param.15, bf16[1,512,512]{1,2,0:T(8,128)(2,1)S(1)} %all_gather.3, bf16[1,512,512]{2,1,0:T(8,128)(2,1)S(1)} %copy-done, bf16[1,512,512]{2,1,0:T(8,128)(2,1)S(1)} %copy-done.5), kind=kOutput, calls=%fused_computation.16 | convolution fusion | flops 538181632 | bytes 3670016 | tf_op jit(solution)/shard_map/kij,kjl->kil/dot_general | solution.py:19
  140.2 2.2 %fusion.9 = bf16[512,512]{1,0:T(8,128)(2,1)S(1)} fusion(f32[1,512,512]{2,1,0:T(8,128)} %fusion.6, bf16[1,512,512]{2,1,0:T(8,128)(2,1)S(1)} %copy-done, bf16[1,512,512]{2,1,0:T(8,128)(2,1)S(1)} %copy-done.5, bf16[1,512,512]{1,2,0:T(8,128)(2,1)S(1)} %add_convert_fusion), kind=kOutput, calls=%fused_computation.19 | convolution fusion | flops 537919488 | bytes 3145728 | tf_op jit(solution)/shard_map/kij,kjl->kil/dot_general | solution.py:19
  142.4 0.9 convolution_convert_fusion.2
  143.3 1.1 broadcast_in_dim.5
  144.4 0.8 constant_dynamic-update-slice_fusion
  145.2 11.2 %all-to-all-start.2 = ((bf16[64,16,512]{2,1,0:T(8,128)(2,1)}), bf16[64,16,512]{2,1,0:T(8,128)(2,1)S(1)}, u32[]{:S(2)}, u32[]{:S(2)}) async-start(bf16[64,16,512]{2,1,0:T(8,128)(2,1)} %constant_dynamic-update-slice_fusion), calls=%async_computation.2 | async-start | bytes 2097152 | tf_op jit(solution)/shard_map/all_to_all | solution.py:101
  156.4 1.0 copy.42
  157.4 0.0 copy-start.1
  157.4 2.8 %fusion.2 = f32[1,512,512]{2,1,0:T(8,128)} fusion(f32[1,512,512]{2,1,0:T(8,128)} %param.12, bf16[1,512,512]{1,2,0:T(8,128)(2,1)S(1)} %all_gather.3), kind=kOutput, calls=%fused_computation.8 | convolution fusion | flops 269221888 | bytes 2621440 | tf_op jit(solution)/shard_map/kij,klj->kil/dot_general | solution.py:19
  160.2 0.0 copy-done.1
  160.2 1.4 fusion.3
  161.6 23.1 %all-to-all-done.2 = bf16[64,16,512]{2,1,0:T(8,128)(2,1)S(1)} async-done(((bf16[64,16,512]{2,1,0:T(8,128)(2,1)}), bf16[64,16,512]{2,1,0:T(8,128)(2,1)S(1)}, u32[]{:S(2)}, u32[]{:S(2)}) %all-to-all-start.2) | async-done | bytes 1048608 | tf_op jit(solution)/shard_map/all_to_all | solution.py:101
  184.7 0.6 copy.47
  185.3 0.4 convolution_convert_fusion.1
  185.7 0.2 copy.48
  185.9 0.8 copy.44
  (2 shorter events, 0.1 us)
Async XLA Ops:
  0.6 136.5 %copy-start = (bf16[1,512,512]{2,1,0:T(8,128)(2,1)S(1)}, bf16[1,512,512]{2,1,0:T(8,128)(2,1)}, u32[]{:S(2)}) copy-start(bf16[1,512,512]{2,1,0:T(8,128)(2,1)} %param.17) | copy-start | bytes 1572868
  0.6 1.9 %copy-start.3 = (s32[64]{0:T(128)S(1)}, s32[64]{0:T(128)}, u32[]{:S(2)}) copy-start(s32[64]{0:T(128)} %param.10) | copy-start | bytes 772
  0.7 1.9 %copy-start.4 = (s32[64]{0:T(128)S(1)}, s32[64]{0:T(128)}, u32[]{:S(2)}) copy-start(s32[64]{0:T(128)} %param.11) | copy-start | bytes 772
  81.3 21.4 %copy-start.2 = (bf16[1,512,512]{2,1,0:T(8,128)(2,1)S(1)}, bf16[1,512,512]{2,1,0:T(8,128)(2,1)}, u32[]{:S(2)}) copy-start(bf16[1,512,512]{2,1,0:T(8,128)(2,1)} %param.14) | copy-start | bytes 1572868
  82.8 54.4 %copy-start.5 = (bf16[1,512,512]{2,1,0:T(8,128)(2,1)S(1)}, bf16[1,512,512]{2,1,0:T(8,128)(2,1)}, u32[]{:S(2)}) copy-start(bf16[1,512,512]{2,1,0:T(8,128)(2,1)} %param.16) | copy-start | bytes 1572868
  82.8 27.4 %all-to-all-start.1 = ((bf16[64,2,256]{2,1,0:T(2,128)(2,1)}), bf16[64,2,256]{2,1,0:T(2,128)(2,1)S(1)}, u32[]{:S(2)}, u32[]{:S(2)}) async-start(bf16[64,2,256]{2,1,0:T(2,128)(2,1)} %reshape.101), calls=%async_computation.1 | async-start | bytes 131072 | tf_op jit(solution)/shard_map/all_to_all | solution.py:81
  145.2 39.5 %all-to-all-start.2 = ((bf16[64,16,512]{2,1,0:T(8,128)(2,1)}), bf16[64,16,512]{2,1,0:T(8,128)(2,1)S(1)}, u32[]{:S(2)}, u32[]{:S(2)}) async-start(bf16[64,16,512]{2,1,0:T(8,128)(2,1)} %constant_dynamic-update-slice_fusion), calls=%async_computation.2 | async-start | bytes 2097152 | tf_op jit(solution)/shard_map/all_to_all | solution.py:101
  157.4 2.8 %copy-start.1 = (f32[1,512,512]{2,1,0:T(8,128)S(1)}, f32[1,512,512]{2,1,0:T(8,128)}, u32[]{:S(2)}) copy-start(f32[1,512,512]{2,1,0:T(8,128)} %param.13) | copy-start | bytes 3145732
where the time goes:
time: 187 us
  blocking collectives  91.3 us (49%)
  waiting for transfers between devices  30.3 us (16%)
  starting transfers between devices  28.4 us (15%)
  local copies, waits for them, and re-layouts  19.7 us (11%)
  matrix products  12.2 us (7%)
  between operations  3.51 us (2%)
    all_to_all x1, blocking collectives, sum_at_owner(): tiles = lax.all_to_all(in_blocks(shard, dim, count), axis, 0, 0, tiled=True)  64.8 us
    all_gather x1, blocking collectives, shards(): grad_blocks = lax.all_gather(jnp.stack(blocks), 'dp', axis=2, tiled=True)  26.5 us
    all_to_all x1, waiting for transfers between devices, shards(): lax.all_to_all(jnp.stack(returned, axis=1).reshape(shard_count * slot_cou...  23.1 us
    all_to_all x1, starting transfers between devices, shards(): lax.all_to_all(share_rows, 'shard', split_axis=0, concat_axis=0, tiled=True)  17.3 us
    unnamed x23, local copies, waits for them, and re-layouts  12.3 us
    all_to_all x1, starting transfers between devices, shards(): lax.all_to_all(jnp.stack(returned, axis=1).reshape(shard_count * slot_cou...  11.2 us
    dot_general x5, matrix products, product(): jnp.einsum(form, left_side, right_side, preferred_element_type=jnp.float32)  10.3 us
    all_to_all x1, waiting for transfers between devices, shards(): lax.all_to_all(share_rows, 'shard', split_axis=0, concat_axis=0, tiled=True)  7.24 us
  transfers between devices with their start and end apart: 2, of which 2 were waited for; matrix products, arithmetic and copies ran while one was open for 3% of the time, Pallas kernels for 0%

commit v1 on v0

v1 whole, which is shorter than its diff:
```python
import functools

import jax
import jax.numpy as jnp
from jax import lax
from jax.experimental import pallas as pl
from jax.experimental.pallas import tpu as pltpu
from jax.sharding import PartitionSpec as P

MESH = pl.DeviceIdType.MESH
F32 = jnp.float32
BF16 = jnp.bfloat16
VMEM_LIMIT = 60 << 20


def dot(a, b):
    return jnp.dot(a, b, preferred_element_type=F32)


def dot_tn(a, b):
    return lax.dot_general(a, b, (((0,), (0,)), ((), ())), preferred_element_type=F32)


def dot_nt(a, b):
    return lax.dot_general(a, b, (((1,), (1,)), ((), ())), preferred_element_type=F32)


class Place:
    def __init__(self, nz, ny, nx):
        self.nz, self.ny, self.nx = nz, ny, nx
        self.z = lax.axis_index("dp")
        self.s = lax.axis_index("shard")
        self.y = self.s // nx
        self.xc = self.s % nx

    def at_z(self, step):
        return ((self.z + self.nz + step) % self.nz, self.s)

    def at_xc(self, xc):
        return (self.z, self.y * self.nx + xc)

    def at_y(self, y):
        return (self.z, y * self.nx + self.xc)

    def slot(self, step):
        return (self.z + 2 * self.nz + step) % self.nz


def enter(at):
    barrier = pltpu.get_barrier_semaphore()

    def signal(peer):
        pl.semaphore_signal(barrier, inc=1, device_id=peer, device_id_type=MESH)

    steps = sorted({abs(child - parent) for parent, child in TREE})
    for step in steps:
        signal(at.at_z(step))
        signal(at.at_z(-step))

    def to_xc(step, carry):
        signal(at.at_xc((at.xc + step) % at.nx))
        return carry

    def to_y(step, carry):
        signal(at.at_y((at.y + step) % at.ny))
        return carry

    lax.fori_loop(1, at.nx, to_xc, 0)
    lax.fori_loop(1, at.ny, to_y, 0)
    pl.semaphore_wait(barrier, 2 * len(steps) + at.nx - 1 + at.ny - 1)


def remote(src, dst, send_sem, recv_sem, peer):
    return pltpu.make_async_remote_copy(
        src_ref=src,
        dst_ref=dst,
        send_sem=send_sem,
        recv_sem=recv_sem,
        device_id=peer,
        device_id_type=MESH,
    )


def swap(count, mine, peer_of, out_buf, in_buf, send_sem, recv_sem, meanwhile=None):
    def start(step, carry):
        j = (mine + step) % count
        remote(out_buf.at[j], in_buf.at[mine], send_sem.at[j], recv_sem.at[mine], peer_of(j)).start()
        return carry

    def finish(step, carry):
        j = (mine + step) % count
        remote(out_buf.at[j], in_buf.at[j], send_sem.at[j], recv_sem.at[j], peer_of(j)).wait_recv()
        return carry

    def drain(step, carry):
        j = (mine + step) % count
        remote(out_buf.at[j], in_buf.at[j], send_sem.at[j], recv_sem.at[j], peer_of(j)).wait_send()
        return carry

    lax.fori_loop(1, count, start, 0)
    in_buf[mine] = out_buf[mine]
    if meanwhile is not None:
        meanwhile()
    lax.fori_loop(1, count, finish, 0)
    return lambda: lax.fori_loop(1, count, drain, 0)


def rows_of(buf, count):
    return jnp.concatenate([buf[j].astype(F32) for j in range(count)], axis=0)


def put_rows(buf, rows, count):
    height = rows.shape[0] // count
    for j in range(count):
        buf[j] = rows[j * height : (j + 1) * height].astype(BF16)


def turned(rows, outer, inner):
    total = outer * inner
    row = lax.broadcasted_iota(jnp.int32, (total, total), 0)
    col = lax.broadcasted_iota(jnp.int32, (total, total), 1)
    pick = (col == (row % outer) * inner + row // outer).astype(F32).astype(BF16)
    return dot(pick, rows.astype(BF16))


def mirrored(right, left):
    edges = []
    for k in range(max(len(right), len(left))):
        edges += right[k : k + 1] + [(-a, -b) for a, b in left[k : k + 1]]
    return tuple(edges)


REACH = [(0, 3), (0, 1), (3, 6), (1, 2), (3, 4), (6, 7), (4, 5)]
TREE = mirrored(REACH + [(7, 8)], REACH)


def children(tree, node):
    return [child for parent, child in tree if parent == node]


def spread(at, tree, buf, send_sem, recv_sem):
    parts = buf.shape[1]

    def edge(parent, child, origin, part):
        ref = buf.at[origin, part]
        sems = send_sem.at[child % at.nz, part], recv_sem.at[child % at.nz, part]
        return remote(ref, ref, *sems, at.at_z(child - parent))

    for part in range(parts):
        for child in children(tree, 0):
            edge(0, child, at.z, part).start()
    for parent, node in tree:
        for part in range(parts):
            edge(parent, node, at.slot(-node), part).wait_recv()
            for child in children(tree, node):
                edge(node, child, at.slot(-node), part).start()
    for parent, child in tree:
        for part in range(parts):
            edge(parent, child, at.slot(-parent), part).wait_send()


def collect(at, tree, x, sums, in_buf, send_sem, recv_sem):
    parts = x.shape[0]

    def edge(parent, child, part):
        inner = children(tree, child)
        src = sums.at[child % at.nz, part] if inner else x.at[part, at.slot(-child)]
        sems = send_sem.at[child % at.nz, part], recv_sem.at[child % at.nz, part]
        return remote(src, in_buf.at[child % at.nz, part], *sems, at.at_z(parent - child))

    def total(node, part):
        value = x[part, at.slot(-node)].astype(F32)
        for child in children(tree, node):
            edge(node, child, part).wait_recv()
            value += in_buf[child % at.nz, part].astype(F32)
        return value

    for parent, child in tree[::-1]:
        if not children(tree, child):
            for part in range(parts):
                edge(parent, child, part).start()
    for parent, child in tree[::-1]:
        if children(tree, child):
            for part in range(parts):
                sums[child % at.nz, part] = total(child, part).astype(BF16)
                edge(parent, child, part).start()

    def drain():
        for parent, child in tree:
            for part in range(parts):
                edge(parent, child, part).wait_send()

    return [total(0, part) for part in range(parts)], drain


def to_owners(at, owner, slot, per_owner):
    count = owner.shape[1]
    shape = (at.nx * at.ny, count)
    row = lax.broadcasted_iota(jnp.int32, shape, 0)
    place = (row % at.ny) * at.nx + row // at.ny
    position = owner[...] * per_owner + slot[...]
    return (place == jnp.broadcast_to(position, shape)).astype(F32).astype(BF16)


def step_kernel(sizes, owner, slot, x_in, *refs):
    fl_in, fr_in, moment_in, second_in, bl_in, br_in = refs[:6]
    out, fl_out, fr_out, moment_out, second_out = refs[6:11]
    x, fl, fr, moment, second, bl, br = loaded = refs[11:18]
    sums, in_sums, held, fl_new, fr_new, moment_new, second_new = refs[18:25]
    out_x, in_x, out_y, in_y, back_x, got_x, back_y, got_y = refs[25:33]
    rs_send, rs_recv, ag_send, ag_recv, last_send, last_recv = refs[33:39]
    x_send, x_recv, y_send, y_recv, bx_send, bx_recv, by_send, by_recv = refs[39:47]
    load_sem, store_sem = refs[47:]
    at = Place(*sizes)
    nz, ny, nx = sizes
    size = bl.shape[-1]
    per_z = size // nz
    half = ny // 2
    cb = out.shape[2]

    stored = (x_in, fl_in, fr_in, moment_in, second_in, bl_in, br_in)
    loads = [
        pltpu.make_async_copy(src, dst, load_sem.at[i])
        for i, (src, dst) in enumerate(zip(stored, loaded))
    ]
    for load in loads:
        load.start()
    enter(at)
    loads[0].wait()
    total, z_drain = collect(at, TREE, x, sums, in_sums, rs_send, rs_recv)

    first_band = at.y < half
    pick = to_owners(at, owner, slot, fl.shape[0])
    none = jnp.zeros_like(total[0])
    placed = []
    for m in range(2):
        placed += [jnp.where(first_band, total[m], none), jnp.where(first_band, none, total[m])]
    put_rows(out_x, dot(pick, jnp.concatenate(placed, axis=0).astype(BF16)), nx)
    x_drain = swap(nx, at.xc, at.at_xc, out_x, in_x, x_send, x_recv)
    put_rows(out_y, turned(rows_of(in_x, nx), nx, ny), ny)
    y_drain = swap(ny, at.y, at.at_y, out_y, in_y, y_send, y_recv)
    mine = [in_y[q].astype(F32) + in_y[q + half].astype(F32) for q in range(half)]
    put_rows(held.at[at.z], jnp.concatenate(mine, axis=0), 2)
    spread(at, TREE, held, ag_send, ag_recv)

    row = lax.broadcasted_iota(jnp.int32, (size, size), 0)
    col = lax.broadcasted_iota(jnp.int32, (size, size), 1)
    order = (col == (row % nz) * per_z + row // nz).astype(F32).astype(BF16)
    g = dot(order, held[...].reshape(size, size)).astype(BF16)
    for load in loads[1:]:
        load.wait()
    left, right = bl[0], br[0]
    rotated = dot(dot_tn(left, g).astype(BF16), right)
    second_next = 0.95 * second[0] + 0.05 * rotated * rotated
    second_new[0] = second_next
    moment_next = (0.9 * moment[0].astype(F32) + 0.1 * g.astype(F32)).astype(BF16)
    moment_new[0] = moment_next
    moment_rotated = dot(dot_tn(left, moment_next).astype(BF16), right)
    scaled = (moment_rotated / (jnp.sqrt(second_next) + 1e-8)).astype(BF16)
    mine = lax.broadcasted_iota(jnp.int32, (per_z, size), 0) * nz + at.z
    rows = (lax.broadcasted_iota(jnp.int32, (per_z, size), 1) == mine).astype(F32).astype(BF16)
    back = dot(dot(rows, left).astype(BF16), scaled).astype(BF16)
    update_rows = dot_nt(back, right)

    stores = [
        pltpu.make_async_copy(src, dst, store_sem.at[i])
        for i, (src, dst) in enumerate(
            (
                (second_new, second_out),
                (moment_new, moment_out),
                (fl_new, fl_out),
                (fr_new, fr_out),
            )
        )
    ]

    def left_factor():
        fl_new[0] = 0.95 * fl[0] + 0.05 * dot_nt(g, g)
        for store in stores[:3]:
            store.start()

    def right_factor():
        fr_new[0] = 0.95 * fr[0] + 0.05 * dot_tn(g, g)
        stores[3].start()

    put_rows(back_y, jnp.concatenate([update_rows, update_rows], axis=0), ny)
    by_drain = swap(ny, at.y, at.at_y, back_y, got_y, by_send, by_recv, left_factor)
    put_rows(back_x, turned(rows_of(got_y, ny), ny, nx), nx)
    bx_drain = swap(nx, at.xc, at.at_xc, back_x, got_x, bx_send, bx_recv, right_factor)
    by_block = dot_tn(pick, rows_of(got_x, nx).astype(BF16))
    for m in range(2):
        first = by_block[2 * m * cb : (2 * m + 1) * cb]
        other = by_block[(2 * m + 1) * cb : (2 * m + 2) * cb]
        out[at.z, m] = jnp.where(first_band, first, other).astype(BF16)
    spread(at, TREE, out, last_send, last_recv)

    z_drain()
    x_drain()
    y_drain()
    by_drain()
    bx_drain()
    for store in stores:
        store.wait()


def dma(*shape):
    return pltpu.SemaphoreType.DMA(shape)


HBM_SPEC = pl.BlockSpec(memory_space=pltpu.HBM)
VMEM_SPEC = pl.BlockSpec(memory_space=pltpu.VMEM)


def step(sizes, owner, slot, x, fl, fr, moment, second, bl, br):
    nz, ny, nx = sizes
    width = x.shape[-1]
    arrays = (x, fl, fr, moment, second, bl, br)
    shares = pltpu.VMEM((nz, 2, ny * nx // 4, width), BF16)
    by_x = pltpu.VMEM((nx, ny, width), BF16)
    by_y = pltpu.VMEM((ny, nx, width), BF16)
    news = (fl, fr, moment, second)
    flops = 14 * width**3
    return pl.pallas_call(
        functools.partial(step_kernel, sizes),
        out_shape=(jax.ShapeDtypeStruct((nz, 2, x.shape[2], width), BF16),)
        + tuple(jax.ShapeDtypeStruct(array.shape, array.dtype) for array in news),
        in_specs=[VMEM_SPEC] * 2 + [HBM_SPEC] * 7,
        out_specs=[VMEM_SPEC] + [HBM_SPEC] * 4,
        scratch_shapes=[pltpu.VMEM(array.shape, array.dtype) for array in arrays]
        + [shares] * 3
        + [pltpu.VMEM(array.shape, array.dtype) for array in news]
        + [by_x, by_x, by_y, by_y] * 2
        + [dma(nz, 2)] * 6
        + [dma(nx), dma(nx), dma(ny), dma(ny)] * 2
        + [dma(7), dma(4)],
        compiler_params=pltpu.CompilerParams(
            collective_id=0, has_side_effects=True, vmem_limit_bytes=VMEM_LIMIT
        ),
        cost_estimate=pl.CostEstimate(
            flops=flops, bytes_accessed=9 << 20, transcendentals=width * width
        ),
    )(owner, slot, *arrays)


def shards(sizes, partials, block_owner, owner_slot, fl, fr, moment, second, bl, br):
    size = bl.shape[-1]
    rows, width = partials.shape[2], partials.shape[3]
    x = partials[0].reshape(2, rows, width // size, size)
    flat = (1, block_owner.shape[0])
    back, *news = step(
        sizes, block_owner.reshape(flat), owner_slot.reshape(flat), x, fl, fr, moment, second, bl, br
    )
    update = jnp.transpose(back, (1, 0, 2, 3)).reshape(2, rows, width)
    return (update, *news)


def solution(mesh):
    nz, shard = mesh.shape["dp"], mesh.shape["shard"]
    nx = 8
    blocks = P("shard", None, None)
    return jax.shard_map(
        functools.partial(shards, (nz, shard // nx, nx)),
        mesh=mesh,
        in_specs=(P("dp", None, "shard", None), P(), P()) + (blocks,) * 6,
        out_specs=(P(None, "shard", None),) + (blocks,) * 4,
        check_vma=False,
    )
```

time: 187 us -> 103 us (0.55)
  blocking collectives: 91.3 us -> 0 us
  Pallas kernels: 0 us -> 90.3 us
  waiting for transfers between devices: 30.3 us -> 0 us
  starting transfers between devices: 28.4 us -> 0 us
  matrix products: 12.2 us -> 0 us
  local copies, waits for them, and re-layouts: 19.7 us -> 9.98 us
  between operations: 3.51 us -> 0.66 us
    pallas_call x0 -> x1, Pallas kernels: none -> 90.3 us  [step(): pl.pallas_call(functools.partial(step_kernel, sizes), out_shape=(jax.Shap...]
    all_to_all x1 -> x0, blocking collectives: 64.8 us -> none  [sum_at_owner(): tiles = lax.all_to_all(in_blocks(shard, dim, count), axis, 0, 0, tiled=True)]
    all_to_all x2 -> x0, waiting for transfers between devices: 30.3 us -> none  [the longest x1 23.1 us: shards(): lax.all_to_all(jnp.stack(returned, axis=1).reshape(shard_count * slot_cou...]
    all_to_all x2 -> x0, starting transfers between devices: 28.4 us -> none  [the longest x1 17.3 us: shards(): lax.all_to_all(share_rows, 'shard', split_axis=0, concat_axis=0, tiled=True)]
    all_gather x1 -> x0, blocking collectives: 26.5 us -> none  [shards(): grad_blocks = lax.all_gather(jnp.stack(blocks), 'dp', axis=2, tiled=True)]
    dot_general x7 -> x0, matrix products: 12.2 us -> none  [the longest x5 10.3 us: product(): jnp.einsum(form, left_side, right_side, preferred_element_type=jnp.float32)]
    unnamed x23 -> x14, local copies, waits for them, and re-layouts: 12.3 us -> 8.47 us
    convert_element_type x1 -> x0, local copies, waits for them, and re-layouts: 2.02 us -> none  [shards(): placed.astype(jnp.bfloat16).reshape(block_count, row_count, block_size)]
  transfers between devices with their start and end apart: 2 -> 0, of which waited for: 2 -> 0; matrix products, arithmetic and copies ran while one was open for 3% -> 0% of each run, Pallas kernels for 0% -> 0%
where the time goes in v1:
time: 103 us; the launch traced here: 101 us
  Pallas kernels  90.3 us (88%)
  local copies, waits for them, and re-layouts  9.98 us (10%)
    pallas_call x1, Pallas kernels, step(): pl.pallas_call(functools.partial(step_kernel, sizes), out_shape=(jax.Shap...  90.3 us
    unnamed x14, local copies, waits for them, and re-layouts  8.47 us

profile of v1, /device:TPU:1, one launch (start us, length us, event | category | flops | bytes accessed | tf_op | source)
XLA Modules:
  0.0 101.0 jit_solution(6690868391874108773)
XLA Ops:
  0.6 2.0 %copy.15 = bf16[4,8,16,512]{3,2,1,0:T(8,128)(2,1)} copy(bf16[4,8,16,512]{3,1,2,0:T(8,128)(2,1)} %bitcast.12) | data formatting | bytes 1048576
  2.6 90.3 %shard_map.128 = (bf16[16,2,16,512]{3,2,1,0:T(8,128)(2,1)}, f32[1,512,512]{2,1,0:T(8,128)}, f32[1,512,512]{2,1,0:T(8,128)}, bf16[1,512,512]{2,1,0:T(8,128)(2,1)}, f32[1,512,512]{2,1,0:T(8,128)}) custom-call(s32[1,64]{1,0:T(1,128)} %bitcast.15, s32[1,64]{1,0:T(1,128)} %bitcast.16, bf16[2,16,16,512]{3,2,1,0:T(8,128)(2,1)} %bitcast.14, f32[1,512,512]{2,1,0:T(8,128)} %refs_0_.1, ...), custom_call_target="tpu_custom_call" | custom-call | flops 1879048192 | bytes 9437184 | tf_op jit(solution)/shard_map/pallas_call | solution.py:323
  93.0 0.0 copy-start.2
  93.0 1.5 %reshape.21 = bf16[2,16,8192]{2,0,1:T(2,128)(2,1)S(1)} reshape(bf16[2,16,16,512]{3,2,0,1:T(8,128)(2,1)} %bitcast.13) | data formatting | bytes 1048576 | tf_op jit(solution)/shard_map/reshape | solution.py:353
  94.5 1.1 %copy.14 = bf16[2,16,8192]{2,1,0:T(8,128)(2,1)} copy(bf16[2,16,8192]{2,0,1:T(2,128)(2,1)S(1)} %reshape.21) | data formatting | bytes 1048576
  95.6 0.0 copy-done.2
  95.6 0.0 copy-start.1
  95.6 1.0 copy.20
  96.6 0.6 copy-done.1
  97.2 0.0 copy-start.3
  97.2 1.0 copy.21
  98.2 0.4 copy-done.3
  98.6 0.0 copy-start
  98.6 0.8 copy.22
  99.4 0.6 copy-done
  100.0 1.0 copy.23
Async XLA Ops:
  93.0 2.6 %copy-start.2 = (f32[1,512,512]{2,1,0:T(8,128)S(1)}, f32[1,512,512]{2,1,0:T(8,128)}, u32[]{:S(2)}) copy-start(f32[1,512,512]{2,1,0:T(8,128)} %get-tuple-element.26) | copy-start | bytes 3145732
  95.6 1.6 %copy-start.1 = (f32[1,512,512]{2,1,0:T(8,128)S(1)}, f32[1,512,512]{2,1,0:T(8,128)}, u32[]{:S(2)}) copy-start(f32[1,512,512]{2,1,0:T(8,128)} %get-tuple-element.27) | copy-start | bytes 3145732
  97.2 1.4 %copy-start.3 = (bf16[1,512,512]{2,1,0:T(8,128)(2,1)S(1)}, bf16[1,512,512]{2,1,0:T(8,128)(2,1)}, u32[]{:S(2)}) copy-start(bf16[1,512,512]{2,1,0:T(8,128)(2,1)} %get-tuple-element.28) | copy-start | bytes 1572868
  98.6 1.4 %copy-start = (f32[1,512,512]{2,1,0:T(8,128)S(1)}, f32[1,512,512]{2,1,0:T(8,128)}, u32[]{:S(2)}) copy-start(f32[1,512,512]{2,1,0:T(8,128)} %get-tuple-element.29) | copy-start | bytes 3145732

commit v2 on v1

--- a/solution.py
+++ b/solution.py
@@ -52,7 +52,7 @@
     def signal(peer):
         pl.semaphore_signal(barrier, inc=1, device_id=peer, device_id_type=MESH)
 
-    steps = sorted({abs(child - parent) for parent, child in TREE})
+    steps = sorted({abs(child - parent) for parent, child in SUM_TREE + TREE})
     for step in steps:
         signal(at.at_z(step))
         signal(at.at_z(-step))
@@ -67,7 +67,7 @@
 
     lax.fori_loop(1, at.nx, to_xc, 0)
     lax.fori_loop(1, at.ny, to_y, 0)
-    pl.semaphore_wait(barrier, 2 * len(steps) + at.nx - 1 + at.ny - 1)
+    return lambda: pl.semaphore_wait(barrier, 2 * len(steps) + at.nx - 1 + at.ny - 1)
 
 
 def remote(src, dst, send_sem, recv_sem, peer):
@@ -130,15 +130,17 @@
     return tuple(edges)
 
 
-REACH = [(0, 3), (0, 1), (3, 6), (1, 2), (3, 4), (6, 7), (4, 5)]
-TREE = mirrored(REACH + [(7, 8)], REACH)
+REACH = [(0, 6), (0, 3), (0, 1), (3, 2), (3, 4), (6, 5), (6, 7)]
+TREE = mirrored(REACH + [(6, 8)], REACH)
+CHAIN = [(0, 3), (0, 1), (3, 6), (1, 2), (3, 4), (6, 7), (4, 5)]
+SUM_TREE = mirrored(CHAIN + [(7, 8)], CHAIN)
 
 
 def children(tree, node):
     return [child for parent, child in tree if parent == node]
 
 
-def spread(at, tree, buf, send_sem, recv_sem):
+def spread(at, tree, buf, send_sem, recv_sem, meanwhile=None):
     parts = buf.shape[1]
 
     def edge(parent, child, origin, part):
@@ -149,6 +151,8 @@
     for part in range(parts):
         for child in children(tree, 0):
             edge(0, child, at.z, part).start()
+    if meanwhile is not None:
+        meanwhile()
     for parent, node in tree:
         for part in range(parts):
             edge(parent, node, at.slot(-node), part).wait_recv()
@@ -159,7 +163,7 @@
             edge(parent, child, at.slot(-parent), part).wait_send()
 
 
-def collect(at, tree, x, sums, in_buf, send_sem, recv_sem):
+def collect(at, tree, x, sums, in_buf, send_sem, recv_sem, prepare):
     parts = x.shape[0]
 
     def edge(parent, child, part):
@@ -175,9 +179,10 @@
             value += in_buf[child % at.nz, part].astype(F32)
         return value
 
-    for parent, child in tree[::-1]:
-        if not children(tree, child):
-            for part in range(parts):
+    for part in range(parts):
+        prepare(part)
+        for parent, child in tree[::-1]:
+            if not children(tree, child):
                 edge(parent, child, part).start()
     for parent, child in tree[::-1]:
         if children(tree, child):
@@ -205,12 +210,12 @@
 def step_kernel(sizes, owner, slot, x_in, *refs):
     fl_in, fr_in, moment_in, second_in, bl_in, br_in = refs[:6]
     out, fl_out, fr_out, moment_out, second_out = refs[6:11]
-    x, fl, fr, moment, second, bl, br = loaded = refs[11:18]
-    sums, in_sums, held, fl_new, fr_new, moment_new, second_new = refs[18:25]
-    out_x, in_x, out_y, in_y, back_x, got_x, back_y, got_y = refs[25:33]
-    rs_send, rs_recv, ag_send, ag_recv, last_send, last_recv = refs[33:39]
-    x_send, x_recv, y_send, y_recv, bx_send, bx_recv, by_send, by_recv = refs[39:47]
-    load_sem, store_sem = refs[47:]
+    flat, fl, fr, moment, second, bl, br = loaded = refs[11:18]
+    x, sums, in_sums, held, fl_new, fr_new, moment_new, second_new, left_by_z, moment_by_z = refs[18:28]
+    out_x, in_x, out_y, in_y, back_x, got_x, back_y, got_y = refs[28:36]
+    rs_send, rs_recv, ag_send, ag_recv, last_send, last_recv = refs[36:42]
+    x_send, x_recv, y_send, y_recv, bx_send, bx_recv, by_send, by_recv = refs[42:50]
+    load_sem, store_sem = refs[50:]
     at = Place(*sizes)
     nz, ny, nx = sizes
     size = bl.shape[-1]
@@ -225,9 +230,16 @@
     ]
     for load in loads:
         load.start()
-    enter(at)
+    entered = enter(at)
     loads[0].wait()
-    total, z_drain = collect(at, TREE, x, sums, in_sums, rs_send, rs_recv)
+
+    def prepare(m):
+        columns = [flat[m, :, c * size : (c + 1) * size] for c in range(cb)]
+        x[m] = turned(jnp.concatenate(columns, axis=0), cb, nz).astype(BF16).reshape(x.shape[1:])
+        if m == 0:
+            entered()
+
+    total, z_drain = collect(at, SUM_TREE, x, sums, in_sums, rs_send, rs_recv, prepare)
 
     first_band = at.y < half
     pick = to_owners(at, owner, slot, fl.shape[0])
@@ -241,25 +253,29 @@
     y_drain = swap(ny, at.y, at.at_y, out_y, in_y, y_send, y_recv)
     mine = [in_y[q].astype(F32) + in_y[q + half].astype(F32) for q in range(half)]
     put_rows(held.at[at.z], jnp.concatenate(mine, axis=0), 2)
-    spread(at, TREE, held, ag_send, ag_recv)
-
     row = lax.broadcasted_iota(jnp.int32, (size, size), 0)
     col = lax.broadcasted_iota(jnp.int32, (size, size), 1)
     order = (col == (row % nz) * per_z + row // nz).astype(F32).astype(BF16)
-    g = dot(order, held[...].reshape(size, size)).astype(BF16)
-    for load in loads[1:]:
-        load.wait()
-    left, right = bl[0], br[0]
-    rotated = dot(dot_tn(left, g).astype(BF16), right)
+    own = lax.broadcasted_iota(jnp.int32, (per_z, size), 0) * nz + at.z
+    rows = (lax.broadcasted_iota(jnp.int32, (per_z, size), 1) == own).astype(F32).astype(BF16)
+
+    def by_z():
+        for load in loads[1:]:
+            load.wait()
+        left_by_z[...] = dot_tn(order, bl[0]).astype(BF16)
+        moment_by_z[...] = dot_tn(order, moment[0]).astype(BF16)
+
+    spread(at, TREE, held, ag_send, ag_recv, by_z)
+
+    g = held[...].reshape(size, size)
+    right = br[0]
+    rotated = dot(dot_tn(left_by_z[...], g).astype(BF16), right)
     second_next = 0.95 * second[0] + 0.05 * rotated * rotated
     second_new[0] = second_next
-    moment_next = (0.9 * moment[0].astype(F32) + 0.1 * g.astype(F32)).astype(BF16)
-    moment_new[0] = moment_next
-    moment_rotated = dot(dot_tn(left, moment_next).astype(BF16), right)
+    moment_next = (0.9 * moment_by_z[...].astype(F32) + 0.1 * g.astype(F32)).astype(BF16)
+    moment_rotated = dot(dot_tn(left_by_z[...], moment_next).astype(BF16), right)
     scaled = (moment_rotated / (jnp.sqrt(second_next) + 1e-8)).astype(BF16)
-    mine = lax.broadcasted_iota(jnp.int32, (per_z, size), 0) * nz + at.z
-    rows = (lax.broadcasted_iota(jnp.int32, (per_z, size), 1) == mine).astype(F32).astype(BF16)
-    back = dot(dot(rows, left).astype(BF16), scaled).astype(BF16)
+    back = dot(dot(rows, bl[0]).astype(BF16), scaled).astype(BF16)
     update_rows = dot_nt(back, right)
 
     stores = [
@@ -275,9 +291,12 @@
     ]
 
     def left_factor():
-        fl_new[0] = 0.95 * fl[0] + 0.05 * dot_nt(g, g)
-        for store in stores[:3]:
-            store.start()
+        stores[0].start()
+        moment_new[0] = dot(order, moment_next).astype(BF16)
+        stores[1].start()
+        ordered = dot(order, g).astype(BF16)
+        fl_new[0] = 0.95 * fl[0] + 0.05 * dot_nt(ordered, ordered)
+        stores[2].start()
 
     def right_factor():
         fr_new[0] = 0.95 * fr[0] + 0.05 * dot_tn(g, g)
@@ -313,7 +332,8 @@
 
 def step(sizes, owner, slot, x, fl, fr, moment, second, bl, br):
     nz, ny, nx = sizes
-    width = x.shape[-1]
+    width = bl.shape[-1]
+    columns = x.shape[2] // width
     arrays = (x, fl, fr, moment, second, bl, br)
     shares = pltpu.VMEM((nz, 2, ny * nx // 4, width), BF16)
     by_x = pltpu.VMEM((nx, ny, width), BF16)
@@ -322,13 +342,15 @@
     flops = 14 * width**3
     return pl.pallas_call(
         functools.partial(step_kernel, sizes),
-        out_shape=(jax.ShapeDtypeStruct((nz, 2, x.shape[2], width), BF16),)
+        out_shape=(jax.ShapeDtypeStruct((nz, 2, columns, width), BF16),)
         + tuple(jax.ShapeDtypeStruct(array.shape, array.dtype) for array in news),
         in_specs=[VMEM_SPEC] * 2 + [HBM_SPEC] * 7,
         out_specs=[VMEM_SPEC] + [HBM_SPEC] * 4,
         scratch_shapes=[pltpu.VMEM(array.shape, array.dtype) for array in arrays]
+        + [pltpu.VMEM((2, nz, columns, width), BF16)]
         + [shares] * 3
         + [pltpu.VMEM(array.shape, array.dtype) for array in news]
+        + [pltpu.VMEM((width, width), BF16)] * 2
         + [by_x, by_x, by_y, by_y] * 2
         + [dma(nz, 2)] * 6
         + [dma(nx), dma(nx), dma(ny), dma(ny)] * 2
@@ -342,16 +364,53 @@
     )(owner, slot, *arrays)
 
 
+def finish_kernel(*refs):
+    stored, outs, here, (update, load_sem, store_sem) = refs[:5], refs[5:10], refs[10:15], refs[15:]
+    back = here[0]
+    loads = [
+        pltpu.make_async_copy(src, dst, load_sem.at[i])
+        for i, (src, dst) in enumerate(zip(stored, here))
+    ]
+    stores = [
+        pltpu.make_async_copy(src, dst, store_sem.at[i])
+        for i, (src, dst) in enumerate(zip((update,) + here[1:], outs))
+    ]
+    for load in loads:
+        load.start()
+    nz, _, cb, size = back.shape
+    loads[0].wait()
+    for m in range(2):
+        by_z = jnp.concatenate([back[z, m] for z in range(nz)], axis=0)
+        by_column = turned(by_z, nz, cb).astype(BF16)
+        for c in range(cb):
+            update[m, :, c * size : (c + 1) * size] = by_column[c * nz : (c + 1) * nz]
+    stores[0].start()
+    for load, store in zip(loads[1:], stores[1:]):
+        load.wait()
+        store.start()
+    for store in stores:
+        store.wait()
+
+
+def finish(back, *news):
+    nz, _, cb, size = back.shape
+    update = jax.ShapeDtypeStruct((2, nz, cb * size), BF16)
+    arrays = (back,) + news
+    return pl.pallas_call(
+        finish_kernel,
+        out_shape=(update,) + tuple(jax.ShapeDtypeStruct(a.shape, a.dtype) for a in news),
+        in_specs=[HBM_SPEC] * 5,
+        out_specs=[HBM_SPEC] * 5,
+        scratch_shapes=[pltpu.VMEM(a.shape, a.dtype) for a in arrays]
+        + [pltpu.VMEM(update.shape, BF16), dma(5), dma(5)],
+        compiler_params=pltpu.CompilerParams(vmem_limit_bytes=VMEM_LIMIT),
+    )(*arrays)
+
+
 def shards(sizes, partials, block_owner, owner_slot, fl, fr, moment, second, bl, br):
-    size = bl.shape[-1]
-    rows, width = partials.shape[2], partials.shape[3]
-    x = partials[0].reshape(2, rows, width // size, size)
     flat = (1, block_owner.shape[0])
-    back, *news = step(
-        sizes, block_owner.reshape(flat), owner_slot.reshape(flat), x, fl, fr, moment, second, bl, br
-    )
-    update = jnp.transpose(back, (1, 0, 2, 3)).reshape(2, rows, width)
-    return (update, *news)
+    owner, slot = block_owner.reshape(flat), owner_slot.reshape(flat)
+    return finish(*step(sizes, owner, slot, partials[0], fl, fr, moment, second, bl, br))
 
 
 def solution(mesh):

time: 103 us -> 95 us (0.922); the launches traced: 101 us -> 94.8 us
  local copies, waits for them, and re-layouts: 9.98 us -> 0 us
  Pallas kernels: 90.3 us -> 94.2 us
    unnamed x14 -> x0, local copies, waits for them, and re-layouts: 8.47 us -> none
    pallas_call x0 -> x1, Pallas kernels: none -> 3.44 us  [finish(): pl.pallas_call(finish_kernel, out_shape=(update,) + tuple((jax.ShapeDtype...]
    reshape x1 -> x0, local copies, waits for them, and re-layouts: 1.52 us -> none  [shards(): update = jnp.transpose(back, (1, 0, 2, 3)).reshape(2, rows, width)]
where the time goes in v2:
time: 95 us; the launch traced here: 94.8 us
  Pallas kernels  94.2 us (99%)
    pallas_call x1, Pallas kernels, step(): pl.pallas_call(functools.partial(step_kernel, sizes), out_shape=(jax.Shap...  90.8 us
    pallas_call x1, Pallas kernels, finish(): pl.pallas_call(finish_kernel, out_shape=(update,) + tuple((jax.ShapeDtype...  3.44 us

profile of v2, /device:TPU:1, one launch (start us, length us, event | category | flops | bytes accessed | tf_op | source)
XLA Modules:
  0.0 94.8 jit_solution(4610664423909885752)
XLA Ops:
  0.6 90.8 %shard_map.128 = (bf16[16,2,16,512]{3,2,1,0:T(8,128)(2,1)}, f32[1,512,512]{2,1,0:T(8,128)}, f32[1,512,512]{2,1,0:T(8,128)}, bf16[1,512,512]{2,1,0:T(8,128)(2,1)}, f32[1,512,512]{2,1,0:T(8,128)}) custom-call(s32[1,64]{1,0:T(1,128)} %bitcast.4, s32[1,64]{1,0:T(1,128)} %bitcast.5, bf16[2,16,8192]{2,1,0:T(8,128)(2,1)} %bitcast.3, f32[1,512,512]{2,1,0:T(8,128)} %refs_0_.1, ...), custom_call_target="tpu_custom_call" | custom-call | flops 1879048192 | bytes 9437184 | tf_op jit(solution)/shard_map/pallas_call | solution.py:343
  91.4 3.4 %shard_map.129 = (bf16[2,16,8192]{2,1,0:T(8,128)(2,1)}, f32[1,512,512]{2,1,0:T(8,128)}, f32[1,512,512]{2,1,0:T(8,128)}, bf16[1,512,512]{2,1,0:T(8,128)(2,1)}, f32[1,512,512]{2,1,0:T(8,128)}) custom-call(bf16[16,2,16,512]{3,2,1,0:T(8,128)(2,1)} %get-tuple-element.10.refs_0_, f32[1,512,512]{2,1,0:T(8,128)} %get-tuple-element.11.refs_1_, ...), custom_call_target="tpu_custom_call" | custom-call | tf_op jit(solution)/shard_map/pallas_call | solution.py:399
